TPU v7x, 32 devices: a whole 2x2x4 slice. The times are simulated.
32 devices in a mesh: groups: 2 (over y), heads: 4 (over z), rows: 4 (over x, core).
Axes of the slice: x: 2, y: 2, z: 4, core: 2. Of those that a mesh axis runs over, the one named last changes fastest.
Arguments:
- queries: bfloat16 [512, 8192], P(('groups', 'heads')), parts along dimension 0, may hold values from -7 to 7
- kv_cache: bfloat16 [2, 4, 16384, 128], P(None, 'groups', ('heads', 'rows')), parts along dimension 1, may hold values from -7 to 7
- start_positions: int32 [4], P('groups'), parts along dimension 0, may hold values from 1024 to 1920, as said below
- residual: bfloat16 [512, 8192], P(('groups', 'heads'), 'rows'), parts along dimension 0, may hold values from -3 to 3
- out_weight: bfloat16 [8192, 8192], P('heads', 'rows'), may hold values from -2 to 2
- norm_gain: float32 [8192], P('rows'), may hold values from 0.1 to 1.9
- gate_weight: bfloat16 [8192, 14336], P('rows', 'heads'), may hold values from -0.0625 to 0.0625
- up_weight: bfloat16 [8192, 14336], P('rows', 'heads'), may hold values from -0.0625 to 0.0625
- down_weight: bfloat16 [14336, 8192], P('heads', 'rows'), may hold values from -0.046875 to 0.046875
Outputs:
- layer_out: bfloat16 [512, 8192], P(('groups', 'heads'), 'rows'), parts along dimension 0
There are 2 independent parts, one for each index of `groups`. A program takes and returns all parts, laid end to end along the dimension named above; an argument that names none is the same for every part. Nothing has to cross between parts.
Inputs may be any that keep to these rules, and one draw needn't show every extreme that they name: Row s * 128 + t of queries is the token at position start_positions[s] + t of sequence s, and the keys and values of the new tokens already stand at those positions of kv_cache; some sequence starts at exactly 1920.
All inputs are finite; a program needn't handle non-finite values.
Results may differ from a plain program's by a relative error of at most 0.017.
Values may be sent and summed in bfloat16 or wider, within the bound.
No kernel may reach another device: no remote copies, remote signals or barrier semaphores. Data moves between devices by JAX's collectives and lax.ppermute only.
A program may use at most 128 MiB of HBM per device.

v0:
```python
import math

import jax
import jax.numpy as jnp
from jax import lax
from jax.sharding import PartitionSpec as P

D = 8192
QH = 64
KVH = 8
HD = 128


NEG_FILL = -1e30
EPSILON = 1e-05


def merged(value, axis, join):
    pieces = jax.tree.map(lambda part: lax.all_gather(part, axis), value)
    head = jax.tree.map(lambda part: part[0], pieces)
    tail = jax.tree.map(lambda part: part[1:], pieces)
    so_far, _ = lax.scan(lambda so_far, section: (join(so_far, section), None), head, tail)
    return so_far


def block_scores(query_block, cache_keys, cache_values, start_positions, first_position):
    new_count = query_block.shape[0] // cache_keys.shape[0]
    score_scale = 1.0 / math.sqrt(cache_keys.shape[2])
    positions = first_position + jnp.arange(cache_keys.shape[1], dtype=jnp.int32)
    maxima = []
    totals = []
    blends = []
    for sequence in range(cache_keys.shape[0]):
        rows_here = query_block[sequence * new_count : (sequence + 1) * new_count]
        scores = (
            jnp.einsum(
                "tkd,pd->ktp", rows_here, cache_keys[sequence], preferred_element_type=jnp.float32
            )
            * score_scale
        )
        last_valid = start_positions[sequence] + jnp.arange(new_count, dtype=jnp.int32)
        allowed = (positions[None, :] <= last_valid[:, None])[None]
        scores = jnp.where(allowed, scores, NEG_FILL)
        row_max = jnp.max(scores, axis=-1)
        weights = jnp.where(allowed, jnp.exp(scores - row_max[..., None]), 0.0)
        maxima.append(jnp.transpose(row_max))
        totals.append(jnp.transpose(jnp.sum(weights, axis=-1)))
        blends.append(
            jnp.einsum(
                "ktp,pd->tkd",
                weights.astype(jnp.bfloat16),
                cache_values[sequence],
                preferred_element_type=jnp.float32,
            )
        )
    return (jnp.concatenate(maxima, 0), jnp.concatenate(totals, 0), jnp.concatenate(blends, 0))


def merge_parts(earlier, later):
    joint = jnp.maximum(earlier[0], later[0])
    early_scale = jnp.exp(earlier[0] - joint)
    late_scale = jnp.exp(later[0] - joint)
    return (
        joint,
        earlier[1] * early_scale + later[1] * late_scale,
        earlier[2] * early_scale[..., None] + later[2] * late_scale[..., None],
    )


def local(
    queries,
    kv_cache,
    start_positions,
    residual,
    out_weight,
    norm_gain,
    gate_weight,
    up_weight,
    down_weight,
):
    head_count = lax.axis_size("heads")
    row_count = lax.axis_size("rows")
    head_index = lax.axis_index("heads")
    row_index = lax.axis_index("rows")
    row_block = queries.shape[0]
    total_rows = row_block * head_count
    group_size = QH // KVH
    per_group = head_count * row_count // KVH
    pos_count = kv_cache.shape[2]
    own_shard = head_index * row_count + row_index
    first_position = own_shard % per_group * pos_count
    shard_ids = jnp.arange(head_count, dtype=jnp.int32) * row_count + row_index
    shard_groups = shard_ids // per_group
    grouped = queries.reshape(row_block, KVH, group_size, HD)
    outgoing = jnp.take(grouped, shard_groups, axis=1)
    row_max, weight_sum, blended = block_scores(
        lax.all_to_all(outgoing, "heads", split_axis=1, concat_axis=0, tiled=True)[:, 0],
        kv_cache[0],
        kv_cache[1],
        start_positions,
        first_position,
    )
    got_max, got_sum, got_blend = (
        lax.all_to_all(
            row_max.reshape(head_count, row_block, group_size),
            "heads",
            split_axis=0,
            concat_axis=0,
            tiled=True,
        ),
        lax.all_to_all(
            weight_sum.reshape(head_count, row_block, group_size),
            "heads",
            split_axis=0,
            concat_axis=0,
            tiled=True,
        ),
        lax.all_to_all(
            blended.reshape(head_count, row_block, group_size, HD),
            "heads",
            split_axis=0,
            concat_axis=0,
            tiled=True,
        ),
    )
    member = (shard_groups[:, None] == jnp.arange(KVH, dtype=jnp.int32)[None, :])[:, None, :, None]
    spread_max = jnp.where(member, got_max[:, :, None, :], NEG_FILL)
    canvas_max = jnp.max(spread_max, axis=0)
    factor = jnp.where(member, jnp.exp(got_max[:, :, None, :] - canvas_max[None]), 0.0)
    canvas_sum = jnp.sum(factor * got_sum[:, :, None, :], axis=0)
    canvas_blend = jnp.einsum("srkg,srgd->rkgd", factor, got_blend, precision=lax.Precision.HIGHEST)
    joint_max, joint_sum, joint_blend = merged(
        (canvas_max, canvas_sum, canvas_blend), "rows", merge_parts
    )
    attended = (
        (joint_blend / joint_sum[..., None]).reshape(row_block, head_count, -1).astype(jnp.bfloat16)
    )
    head_rows = lax.all_to_all(attended, "heads", split_axis=1, concat_axis=0, tiled=True).reshape(
        total_rows, -1
    )
    row_start = head_index * row_block
    local_term = jnp.dot(head_rows, out_weight, preferred_element_type=jnp.float32)
    own_rows = lax.dynamic_slice_in_dim(local_term, row_start, row_block, 0) + residual.astype(
        jnp.float32
    )
    local_term = lax.dynamic_update_slice_in_dim(local_term, own_rows, row_start, 0)
    resid_all = lax.psum(local_term, "heads").astype(jnp.bfloat16)
    resid_own = lax.dynamic_slice_in_dim(resid_all, row_start, row_block, 0)
    resid_wide = resid_all.astype(jnp.float32)
    square = jnp.sum(resid_wide * resid_wide, axis=1)
    scaled = (resid_wide * norm_gain).astype(jnp.bfloat16)
    gate_part = jnp.dot(scaled, gate_weight, preferred_element_type=jnp.float32)
    up_part = jnp.dot(scaled, up_weight, preferred_element_type=jnp.float32)
    gate_sum, up_sum, square_sum = lax.psum((gate_part, up_part, square), "rows")
    inverse = lax.rsqrt(square_sum / D + EPSILON)[:, None]
    hidden = (jax.nn.silu(gate_sum * inverse) * (up_sum * inverse)).astype(jnp.bfloat16)
    down_sum = lax.psum_scatter(
        jnp.dot(hidden, down_weight, preferred_element_type=jnp.float32),
        "heads",
        scatter_dimension=0,
        tiled=True,
    )
    return (resid_own.astype(jnp.float32) + down_sum).astype(jnp.bfloat16)


def solution(mesh):
    return jax.shard_map(
        local,
        mesh=mesh,
        in_specs=(
            P(("groups", "heads"), None),
            P(None, "groups", ("heads", "rows"), None),
            P("groups"),
            P(("groups", "heads"), "rows"),
            P("heads", "rows"),
            P("rows"),
            P("rows", "heads"),
            P("rows", "heads"),
            P("heads", "rows"),
        ),
        out_specs=P(("groups", "heads"), "rows"),
        check_vma=False,
    )
```

profile of v0, /device:TPU:0, one launch (start us, length us, event | category | flops | bytes accessed | tf_op | source)
XLA Modules:
  0.0 497.8 jit_solution(7816099900571446197)
XLA Ops:
  6.6 1.6 copy.90
  8.2 0.8 gather_fusion
  8.9 0.9 select_bitcast_fusion
  9.8 6.3 %all-to-all-start = ((bf16[64,4,8,128]{3,2,0,1:T(8,128)(2,1)}), bf16[64,4,8,128]{3,2,0,1:T(8,128)(2,1)S(1)}, u32[]{:S(2)}, u32[]{:S(2)}) async-start(bf16[64,4,8,128]{3,2,0,1:T(8,128)(2,1)} %select_bitcast_fusion), calls=%async_computation | async-start | bytes 1048576 | tf_op jit(solution)/shard_map/all_to_all | solution.py:97
  16.2 0.7 fusion.60
  16.8 0.6 iota_add_fusion.2
  17.5 0.7 iota_add_fusion.1
  18.2 0.2 broadcast_compare_fusion.1
  18.4 12.2 %all-to-all-done = bf16[64,4,8,128]{3,2,0,1:T(8,128)(2,1)S(1)} async-done(((bf16[64,4,8,128]{3,2,0,1:T(8,128)(2,1)}), bf16[64,4,8,128]{3,2,0,1:T(8,128)(2,1)S(1)}, u32[]{:S(2)}, u32[]{:S(2)}) %all-to-all-start) | async-done | bytes 524320 | tf_op jit(solution)/shard_map/all_to_all | solution.py:97
  30.8 0.9 bitcast_reduce_fusion
  31.8 1.3 fusion.27
  33.1 0.6 copy-done
  33.7 0.9 bitcast_reduce_fusion.1
  34.7 1.3 fusion.24
  36.0 0.7 copy-done.1
  36.7 0.7 reshape.225
  37.4 3.2 all-to-all-start.1
  40.7 1.6 copy.75
  42.3 3.9 all-to-all-done.1
  46.2 3.5 all-to-all-start.3
  49.7 0.2 all-gather.5.cloned.1.call-start
  50.1 0.5 broadcast.272
  50.6 0.6 reduce
  51.3 0.2 copy.70
  51.5 0.8 select_reduce_fusion
  52.3 21.5 %all-to-all-done.3 = f32[4,64,8,128]{3,2,1,0:T(8,128)S(1)} async-done(((f32[4,64,8,128]{3,2,1,0:T(8,128)}), f32[4,64,8,128]{3,2,1,0:T(8,128)S(1)}, u32[]{:S(2)}, u32[]{:S(2)}) %all-to-all-start.3) | async-done | bytes 1048608 | tf_op jit(solution)/shard_map/all_to_all | solution.py:118
  73.8 5.3 %convolution_bitcast_fusion = f32[64,8,8,128]{3,1,2,0:T(8,128)S(1)} fusion(f32[4,64,8,128]{3,2,1,0:T(8,128)S(1)} %all-to-all-done.3, f32[64,8,8]{1,2,0:T(8,128)S(1)} %select_reduce_fusion, f32[4,64,8]{0,2,1:T(8,128)S(1)} %copy.70, pred[4,8]{1,0:T(4,128)(4,1)S(1)} %iota_compare_fusion), kind=kOutput, calls=%fused_computation.38 | convolution fusion | flops 25198592 | bytes 3170336 | tf_op jit(solution)/shard_map/srkg,srgd->rkgd/dot_general | solution.py:131
  79.1 1.8 copy.77
  80.9 4.9 fusion.8
  85.9 0.7 reshape.227
  86.6 3.3 all-to-all-start.2
  90.0 16.2 %all-gather = f32[256,8,8]{2,1,0:T(8,128)S(1)} all-gather(f32[64,8,8]{2,1,0:T(8,128)S(1)} %copy.71), channel_id=2, replica_groups=mesh['groups'=2,'heads'=4,'rows'=4] {'rows'}, dimensions={0}, use_global_device_ids=true | all-gather | bytes 81920 | tf_op jit(solution)/shard_map/all_gather | solution.py:19
  106.3 0.6 reduce.1
  107.0 0.2 copy.73
  107.2 1.3 multiply_reduce_fusion
  108.6 16.4 %all-gather.1 = f32[256,8,8]{2,1,0:T(8,128)S(1)} all-gather(f32[64,8,8]{2,1,0:T(8,128)S(1)} %copy.74), channel_id=3, replica_groups=mesh['groups'=2,'heads'=4,'rows'=4] {'rows'}, dimensions={0}, use_global_device_ids=true | all-gather | bytes 81920 | tf_op jit(solution)/shard_map/all_gather | solution.py:19
  125.2 0.3 copy.82
  125.6 0.3 copy.83
  125.9 23.8 %all-gather.5.cloned.1.call-done = f32[256,8,8,128]{3,2,1,0:T(8,128)} async-done(((f32[64,8,8,128]{3,2,1,0:T(8,128)}), f32[256,8,8,128]{3,2,1,0:T(8,128)}) %all-gather.5.cloned.1.call-update) | async-done | bytes 8388624 | tf_op jit(solution)/shard_map/all_gather | solution.py:19
  149.7 6.8 %slice.89 = f32[192,8,8,128]{3,2,1,0:T(8,128)} slice(f32[256,8,8,128]{3,2,1,0:T(8,128)} %all-gather.5.cloned.1.call-done), slice={[64:256], [0:8], [0:8], [0:128]} | slice | bytes 12582912 | tf_op jit(solution)/shard_map/slice | solution.py:21
  156.5 9.2 %while.14 = (s32[]{:T(128)}, f32[64,8,8]{0,2,1:T(8,128)S(1)}, f32[64,8,8]{0,2,1:T(8,128)S(1)}, f32[64,8,8,128]{3,2,1,0:T(8,128)S(1)}, f32[3,64,8,8]{1,3,2,0:T(8,...) while((s32[]{:T(128)}, f32[64,8,8]{0,2,1:T(8,128)S(1)}, ...), condition=%wide.region_7.8_spmd, body=%wide.region_6.7_spmd.sunk | while | flops 1597442 | bytes 6520933 | solution.py:22
  156.5 0.1 copy.99
  156.7 0.1 copy.100
  156.8 2.7 fusion.72
  159.6 0.1 copy.99
  159.7 0.1 copy.100
  159.9 2.7 fusion.72
  162.6 0.1 copy.99
  162.9 2.7 fusion.72
  165.8 0.7 divide_convert_fusion
  166.5 0.3 convert_element_type.36
  166.8 1.6 copy.85
  168.4 4.6 all-to-all-start.4
  173.0 26.1 %all-to-all-done.4 = bf16[64,4,2048]{2,0,1:T(8,128)(2,1)S(1)} async-done(((bf16[64,4,2048]{2,0,1:T(8,128)(2,1)}), bf16[64,4,2048]{2,0,1:T(8,128)(2,1)S(1)}, u32[]{:S(2)}, u32[]{:S(2)}) %all-to-all-start.4) | async-done | bytes 1048608 | tf_op jit(solution)/shard_map/all_to_all | solution.py:138
  199.1 5.7 %fusion.61 = f32[256,2048]{1,0:T(8,128)S(1)} fusion(bf16[256,2048]{1,0:T(8,128)(2,1)S(1)} %bitcast.134, bf16[2048,2048]{1,0:T(8,128)(2,1)} %param.15), kind=kOutput, calls=%fused_computation.99 | convolution fusion | flops 2147483648 | bytes 11534336 | tf_op jit(solution)/shard_map/dot_general | solution.py:142
  205.0 73.8 %all-reduce.5 = bf16[256,2048]{1,0:T(8,128)(2,1)S(1)} all-reduce(f32[256,2048]{1,0:T(8,128)S(1)} %add_dynamic-update-slice_fusion), channel_id=1, replica_groups=mesh['groups'=2,'heads'=4,'rows'=4] {'heads'}, use_global_device_ids=true, to_apply=%region_8.9 | all-reduce | flops 524288 | bytes 3145728 | tf_op jit(solution)/shard_map/psum | solution.py:147
  278.9 9.2 %fusion.33 = f32[256,3584]{1,0:T(8,128)} fusion(bf16[2048,3584]{1,0:T(8,128)(2,1)} %param.17, bf16[256,2048]{1,0:T(8,128)(2,1)S(1)} %all-reduce.5, f32[2048]{0:T(1024)S(1)} %copy-done.5), kind=kOutput, calls=%fused_computation.47 | convolution fusion | flops 3759669248 | bytes 19406848 | tf_op jit(solution)/shard_map/dot_general | solution.py:152
  288.0 9.1 %fusion.31 = f32[256,3584]{1,0:T(8,128)} fusion(bf16[2048,3584]{1,0:T(8,128)(2,1)} %param.18, bf16[256,2048]{1,0:T(8,128)(2,1)S(1)} %all-reduce.5, f32[2048]{0:T(1024)S(1)} %copy-done.5), kind=kOutput, calls=%fused_computation.46 | convolution fusion | flops 3759669248 | bytes 19406848 | tf_op jit(solution)/shard_map/dot_general | solution.py:153
  297.2 0.3 fusion.12
  297.5 6.2 %psum.30 = f32[256]{0:T(256)S(1)} all-reduce(f32[256]{0:T(256)S(1)} %fusion.12), channel_id=1, replica_groups=mesh['groups'=2,'heads'=4,'rows'=4] {'rows'}, use_global_device_ids=true, to_apply=%region_11.12 | all-reduce | flops 256 | bytes 2048 | tf_op jit(solution)/shard_map/psum | solution.py:154
  303.7 128.7 %all-reduce.4.cloned.1.call-done = (f32[256,3584]{1,0:T(8,128)}, f32[256,3584]{1,0:T(8,128)}) async-done(((f32[256,3584]{1,0:T(8,128)}, f32[256,3584]{1,0:T(8,128)}), (f32[256,3584]{1,0:T(8,128)}, f32[256,3584]{1,0:T(8,128)})) %all-reduce.4.cloned.1.call-update) | async-done | bytes 7340048 | tf_op jit(solution)/shard_map/psum | solution.py:154
  432.4 13.0 %fusion.21 = f32[256,2048]{1,0:T(8,128)} fusion(bf16[3584,2048]{1,0:T(8,128)(2,1)} %param.19, f32[256,3584]{1,0:T(8,128)} %get-tuple-element.94, f32[256,3584]{1,0:T(8,128)} %get-tuple-element.95, f32[256]{0:T(256)S(1)} %add_rsqrt_fusion), kind=kOutput, calls=%fused_computation.35 | convolution fusion | flops 3765436416 | bytes 24118272 | tf_op jit(solution)/shard_map/dot_general | solution.py:158
  445.4 44.0 %reduce-scatter.2.cloned.1.call-done = f32[64,2048]{1,0:T(8,128)} async-done(((f32[256,2048]{1,0:T(8,128)}), f32[64,2048]{1,0:T(8,128)}) %reduce-scatter.2.cloned.1.call-update) | async-done | bytes 524304 | tf_op jit(solution)/shard_map/reduce_scatter | solution.py:157
  489.5 1.8 add_convert_fusion
  (51 shorter events, 1.9 us)
Async XLA Ops:
  6.5 9.6 %copy-start.4 = (s32[2]{0:T(128)S(1)}, s32[2]{0:T(128)}, u32[]{:S(2)}) copy-start(s32[2]{0:T(128)} %param.13) | copy-start | bytes 28
  6.5 24.3 %copy-start.2 = (bf16[2,2,1024,128]{3,2,1,0:T(8,128)(2,1)S(1)}, bf16[2,2,1024,128]{3,2,1,0:T(8,128)(2,1)}, u32[]{:S(2)}) copy-start(bf16[2,2,1024,128]{3,2,1,0:T(8,128)(2,1)} %param.12) | copy-start | bytes 3145732
  9.8 20.8 %all-to-all-start = ((bf16[64,4,8,128]{3,2,0,1:T(8,128)(2,1)}), bf16[64,4,8,128]{3,2,0,1:T(8,128)(2,1)S(1)}, u32[]{:S(2)}, u32[]{:S(2)}) async-start(bf16[64,4,8,128]{3,2,0,1:T(8,128)(2,1)} %select_bitcast_fusion), calls=%async_computation | async-start | bytes 1048576 | tf_op jit(solution)/shard_map/all_to_all | solution.py:97
  31.8 2.0 copy-start
  34.7 2.0 copy-start.1
  37.4 8.8 %all-to-all-start.1 = ((f32[4,1,512]{2,1,0:T(1,128)}), f32[4,1,512]{2,1,0:T(1,128)S(1)}, u32[]{:S(2)}, u32[]{:S(2)}) async-start(f32[4,1,512]{2,1,0:T(1,128)} %reshape.225), calls=%async_computation.1 | async-start | bytes 16384 | tf_op jit(solution)/shard_map/all_to_all | solution.py:104
  46.2 27.6 %all-to-all-start.3 = ((f32[4,64,8,128]{3,2,1,0:T(8,128)}), f32[4,64,8,128]{3,2,1,0:T(8,128)S(1)}, u32[]{:S(2)}, u32[]{:S(2)}) async-start(f32[4,64,8,128]{3,2,1,0:T(8,128)} %copy.75), calls=%async_computation.3 | async-start | bytes 2097152 | tf_op jit(solution)/shard_map/all_to_all | solution.py:118
  49.7 100.0 %all-gather.5.cloned.1.call-start = ((), (), s32[]{:S(2)}) async-start(), calls=%async_computation.7 | async-start | bytes 10485760 | tf_op jit(solution)/shard_map/all_gather | solution.py:19
  86.6 19.6 %all-to-all-start.2 = ((f32[4,1,512]{2,1,0:T(1,128)}), f32[4,1,512]{2,1,0:T(1,128)S(1)}, u32[]{:S(2)}, u32[]{:S(2)}) async-start(f32[4,1,512]{2,1,0:T(1,128)} %reshape.227), calls=%async_computation.2 | async-start | bytes 16384 | tf_op jit(solution)/shard_map/all_to_all | solution.py:111
  149.7 6.8 %slice-start = ((f32[256,8,8,128]{3,2,1,0:T(8,128)}), f32[64,8,8,128]{3,2,1,0:T(8,128)S(1)}, s32[]{:S(2)}) async-start(f32[256,8,8,128]{3,2,1,0:T(8,128)} %all-gather.5.cloned.1.call-done), calls=%async_computation.9 | async-start | bytes 4194304 | tf_op jit(solution)/shard_map/slice | solution.py:20
  168.4 30.7 %all-to-all-start.4 = ((bf16[64,4,2048]{2,0,1:T(8,128)(2,1)}), bf16[64,4,2048]{2,0,1:T(8,128)(2,1)S(1)}, u32[]{:S(2)}, u32[]{:S(2)}) async-start(bf16[64,4,2048]{2,0,1:T(8,128)(2,1)} %copy.85), calls=%async_computation.4 | async-start | bytes 2097152 | tf_op jit(solution)/shard_map/all_to_all | solution.py:138
  173.0 259.4 %all-reduce.4.cloned.1.call-start = ((), (), s32[]{:S(2)}) async-start(), calls=%async_computation.8 | async-start | bytes 14680064 | tf_op jit(solution)/shard_map/psum | solution.py:154
  199.1 5.8 %copy-start.3 = (bf16[64,2048]{1,0:T(8,128)(2,1)S(1)}, bf16[64,2048]{1,0:T(8,128)(2,1)}, u32[]{:S(2)}) copy-start(bf16[64,2048]{1,0:T(8,128)(2,1)} %param.14) | copy-start | bytes 786436
  204.9 73.9 %copy-start.5 = (f32[2048]{0:T(1024)S(1)}, f32[2048]{0:T(1024)}, u32[]{:S(2)}) copy-start(f32[2048]{0:T(1024)} %param.16) | copy-start | bytes 24580
  297.2 192.3 %reduce-scatter.2.cloned.1.call-start = ((), (), s32[]{:S(2)}) async-start(), calls=%async_computation.6 | async-start | bytes 2621440 | tf_op jit(solution)/shard_map/reduce_scatter | solution.py:157
Sparse Core Ops, SparseCore 0:
  81.0 68.6 all-gather.4
  297.3 135.0 all-reduce.3
  445.5 43.8 reduce-scatter.1
where the time goes:
time: 498 us
  waiting for transfers between devices  260 us (52%)
  blocking collectives  113 us (23%)
  matrix products  46.7 us (9%)
  other arithmetic  22 us (4%)
  local copies, waits for them, and re-layouts  21.3 us (4%)
  starting transfers between devices  21.2 us (4%)
  between operations  13.4 us (3%)
    psum x1, waiting for transfers between devices, local(): lax.psum((gate_part, up_part, square), 'rows')  129 us
    psum x1, blocking collectives, local(): resid_all = lax.psum(local_term, 'heads').astype(jnp.bfloat16)  73.8 us
    reduce_scatter x1, waiting for transfers between devices, local(): lax.psum_scatter(jnp.dot(hidden, down_weight, preferred_element_type=jnp....  44 us
    all_gather x2, blocking collectives, merged(): pieces = jax.tree.map(lambda part: lax.all_gather(part, axis), value)  32.6 us
    all_to_all x1, waiting for transfers between devices, local(): lax.all_to_all(attended, 'heads', split_axis=1, concat_axis=0, tiled=True)  26.1 us
    all_gather x1, waiting for transfers between devices, merged(): pieces = jax.tree.map(lambda part: lax.all_gather(part, axis), value)  23.8 us
    all_to_all x1, waiting for transfers between devices, local(): lax.all_to_all(blended.reshape(head_count, row_block, group_size, HD), 'h...  21.5 us
    dot_general x1, matrix products, local(): jnp.dot(hidden, down_weight, preferred_element_type=jnp.float32)  13 us
  transfers between devices with their start and end apart: 8, of which 7 were waited for; matrix products, arithmetic and copies ran while one was open for 3% of the time, Pallas kernels for 0%

commit v1 on v0

--- a/solution.py
+++ b/solution.py
@@ -1,8 +1,11 @@
+import functools
 import math
 
 import jax
 import jax.numpy as jnp
 from jax import lax
+from jax.experimental import pallas as pl
+from jax.experimental.pallas import tpu as pltpu
 from jax.sharding import PartitionSpec as P
 
 D = 8192
@@ -13,6 +16,17 @@
 
 NEG_FILL = -1e30
 EPSILON = 1e-05
+
+CORE_SWAP = [(0, 1), (1, 0), (2, 3), (3, 2)]
+CHIP_SWAP = [(0, 2), (2, 0), (1, 3), (3, 1)]
+TO_CENTRE = [(0, 1), (3, 2)]
+CENTRE_SWAP = [(1, 2), (2, 1)]
+FROM_CENTRE = [(1, 0), (2, 3)]
+VMEM_BYTES = 56 << 20
+
+ANY = pl.BlockSpec(memory_space=pl.ANY)
+VMEM = pl.BlockSpec(memory_space=pltpu.VMEM)
+SMEM = pl.BlockSpec(memory_space=pltpu.SMEM)
 
 
 def merged(value, axis, join):
@@ -67,7 +81,7 @@
     )
 
 
-def local(
+def general_local(
     queries,
     kv_cache,
     start_positions,
@@ -163,7 +177,307 @@
     return (resid_own.astype(jnp.float32) + down_sum).astype(jnp.bfloat16)
 
 
+def params():
+    return pltpu.CompilerParams(vmem_limit_bytes=VMEM_BYTES)
+
+
+def attention_kernel(info, starts, q, near, far, out):
+    sequences, positions, depth = near.shape[1:]
+    new_count = q.shape[0] // sequences
+    heads = q.shape[1] // depth
+    scale = 1.0 / math.sqrt(depth)
+    core = info[2]
+    shape = (heads * new_count, positions)
+    token = lax.broadcasted_iota(jnp.int32, shape, 0) & (new_count - 1)
+    column = lax.broadcasted_iota(jnp.int32, shape, 1)
+    for s in range(sequences):
+        rows = slice(s * new_count, (s + 1) * new_count)
+        stacked = jnp.concatenate(
+            [q[rows, k * depth : (k + 1) * depth] for k in range(heads)], axis=0
+        )
+        last = starts[s] + token
+        scores = []
+        for half, block in ((core, near), (1 - core, far)):
+            raw = lax.dot_general(
+                stacked, block[0, s], (((1,), (1,)), ((), ())), preferred_element_type=jnp.float32
+            )
+            scores.append(jnp.where(column + half * positions <= last, raw * scale, NEG_FILL))
+        top = jnp.maximum(
+            jnp.max(scores[0], axis=1, keepdims=True), jnp.max(scores[1], axis=1, keepdims=True)
+        )
+        total = 0.0
+        blend = 0.0
+        for half, block, score in ((core, near, scores[0]), (1 - core, far, scores[1])):
+            weight = jnp.where(column + half * positions <= last, jnp.exp(score - top), 0.0)
+            total += jnp.sum(weight, axis=1, keepdims=True)
+            blend += jnp.dot(
+                weight.astype(jnp.bfloat16), block[1, s], preferred_element_type=jnp.float32
+            )
+        result = (blend / total).astype(out.dtype)
+        for k in range(heads):
+            out[rows, k * depth : (k + 1) * depth] = result[k * new_count : (k + 1) * new_count]
+
+
+def attention(info, starts, q, near, far):
+    return pl.pallas_call(
+        attention_kernel,
+        out_shape=jax.ShapeDtypeStruct(q.shape, jnp.bfloat16),
+        in_specs=[SMEM, SMEM, VMEM, VMEM, VMEM],
+        out_specs=VMEM,
+        compiler_params=params(),
+        name="attention",
+    )(info, starts, q, near, far)
+
+
+def project_kernel(first, info, own, core, chip, cross, residual, w_hbm, out, w, total, sem):
+    depth = own.shape[1]
+    width = out.shape[1]
+    pieces = (own, core, chip, cross)
+    copies = []
+    for j in range(4):
+        row = pl.multiple_of((info[1] ^ j) * depth, depth)
+        copy = pltpu.make_async_copy(
+            w_hbm.at[pl.ds(row, depth), pl.ds(first, width)], w.at[j], sem.at[j]
+        )
+        copy.start()
+        copies.append(copy)
+    for j in range(4):
+        copies[j].wait()
+        product = jnp.dot(pieces[j][...], w[j], preferred_element_type=jnp.float32)
+        if j == 0:
+            total[...] = product
+        else:
+            total[...] += product
+    block = residual.shape[0]
+    mine = pl.ds(pl.multiple_of(info[0] * block, block), block)
+    total[mine] += residual[:, first : first + width].astype(jnp.float32)
+    for k in range(4):
+        source = pl.ds(pl.multiple_of((info[4] ^ k) * block, block), block)
+        out[k * block : (k + 1) * block] = total[source].astype(out.dtype)
+
+
+def project(info, pieces, residual, weight, first, width):
+    rows, depth = pieces[0].shape
+    return pl.pallas_call(
+        functools.partial(project_kernel, first),
+        out_shape=jax.ShapeDtypeStruct((rows, width), jnp.bfloat16),
+        in_specs=[SMEM] + [VMEM] * 5 + [ANY],
+        out_specs=VMEM,
+        scratch_shapes=[
+            pltpu.VMEM((4, depth, width), jnp.bfloat16),
+            pltpu.VMEM((rows, width), jnp.float32),
+            pltpu.SemaphoreType.DMA((4,)),
+        ],
+        compiler_params=params(),
+        name="project",
+    )(info, *pieces, residual, weight)
+
+
+def expand_kernel(first, step, parts, gain, *refs):
+    resid = refs[:parts]
+    gate_hbm, up_hbm, keep, send, square, scaled, w, sem = refs[parts:]
+    count = keep.shape[1] // (2 * step)
+    half = keep.shape[0]
+    copies = []
+    for i in range(count):
+        for j, source in enumerate((gate_hbm, up_hbm)):
+            copy = pltpu.make_async_copy(
+                source.at[:, pl.ds(first + i * step, step)], w.at[i, j], sem.at[i, j]
+            )
+            copy.start()
+            copies.append(copy)
+    width = resid[0].shape[1]
+    total = None
+    for p in range(parts):
+        wide = resid[p][...].astype(jnp.float32)
+        piece = jnp.sum(wide * wide, axis=1, keepdims=True)
+        total = piece if total is None else total + piece
+        columns = slice(p * width, (p + 1) * width)
+        scaled[:, columns] = (wide * gain[:, columns]).astype(jnp.bfloat16)
+    square[...] = jnp.broadcast_to(total, square.shape)
+    for i in range(count):
+        for j in range(2):
+            copies[2 * i + j].wait()
+            product = jnp.dot(scaled[...], w[i, j], preferred_element_type=jnp.float32)
+            product = product.astype(keep.dtype)
+            columns = slice((j * count + i) * step, (j * count + i + 1) * step)
+            keep[:, columns] = product[:half]
+            send[:, columns] = product[half:]
+
+
+def expand(resid, gain, gate_weight, up_weight, first, width, step):
+    rows = resid[0].shape[0]
+    parts = len(resid)
+    depth = gate_weight.shape[0]
+    half = jax.ShapeDtypeStruct((rows // 2, 2 * width), jnp.bfloat16)
+    return pl.pallas_call(
+        functools.partial(expand_kernel, first, step, parts),
+        out_shape=(half, half, jax.ShapeDtypeStruct((rows, HD), jnp.float32)),
+        in_specs=[VMEM] * (1 + parts) + [ANY, ANY],
+        out_specs=(VMEM, VMEM, VMEM),
+        scratch_shapes=[
+            pltpu.VMEM((rows, depth), jnp.bfloat16),
+            pltpu.VMEM((width // step, 2, depth, step), jnp.bfloat16),
+            pltpu.SemaphoreType.DMA((width // step, 2)),
+        ],
+        compiler_params=params(),
+        name="expand",
+    )(gain, *resid, gate_weight, up_weight)
+
+
+def contract_kernel(first, step, final, info, *refs):
+    if final:
+        own, chip, core, before, w_hbm, out, hidden, w, total, sem = refs
+    else:
+        own, chip, core, w_hbm, out, hidden, w, sem = refs
+        total = out
+    block = own.shape[0]
+    count = own.shape[1] // step
+    copies = []
+    for i in range(count):
+        copy = pltpu.make_async_copy(
+            w_hbm.at[pl.ds(first + i * step, step)], w.at[i], sem.at[i]
+        )
+        copy.start()
+        copies.append(copy)
+    hidden[:block] = own[...]
+    hidden[block : 2 * block] = chip[...]
+    hidden[2 * block :] = core[...]
+    for i in range(count):
+        copies[i].wait()
+        product = jnp.dot(
+            hidden[:, i * step : (i + 1) * step], w[i], preferred_element_type=jnp.float32
+        )
+        if i > 0:
+            total[...] += product
+        elif final:
+            total[...] = before[...] + product
+        else:
+            total[...] = product
+    if final:
+        for k in range(4):
+            source = pl.ds(pl.multiple_of((info[4] ^ k) * block, block), block)
+            out[k] = total[source].astype(out.dtype)
+
+
+def contract(info, hidden, before, weight, first, step):
+    own, chip, core = hidden
+    block, width = own.shape
+    rows = 4 * block
+    columns = weight.shape[1]
+    final = before is not None
+    if final:
+        out_shape = jax.ShapeDtypeStruct((4, block, columns), jnp.bfloat16)
+    else:
+        out_shape = jax.ShapeDtypeStruct((rows, columns), jnp.float32)
+    scratch = [
+        pltpu.VMEM((rows, width), jnp.bfloat16),
+        pltpu.VMEM((width // step, step, columns), jnp.bfloat16),
+    ]
+    if final:
+        scratch.append(pltpu.VMEM((rows, columns), jnp.float32))
+    scratch.append(pltpu.SemaphoreType.DMA((width // step,)))
+    arrays = [own, chip, core] + ([before] if final else [])
+    return pl.pallas_call(
+        functools.partial(contract_kernel, first, step, final),
+        out_shape=out_shape,
+        in_specs=[SMEM] + [VMEM] * len(arrays) + [ANY],
+        out_specs=VMEM,
+        scratch_shapes=scratch,
+        compiler_params=params(),
+        name="contract",
+    )(info, *arrays, weight)
+
+
+def wide_sum(*values):
+    total = values[0].astype(jnp.float32)
+    for value in values[1:]:
+        total = total + value.astype(jnp.float32)
+    return total
+
+
+def block_local(
+    queries,
+    kv_cache,
+    start_positions,
+    residual,
+    out_weight,
+    norm_gain,
+    gate_weight,
+    up_weight,
+    down_weight,
+):
+    z = lax.axis_index("heads")
+    r = lax.axis_index("rows")
+    core = r % 2
+    chip = r // 2
+    info = jnp.stack([z, r, core, chip, 2 * core + chip]).astype(jnp.int32)
+    at_end = (z == 0) | (z == 3)
+    row_block = queries.shape[0]
+    far = lax.ppermute(kv_cache, "rows", CORE_SWAP)
+    outgoing = lax.dynamic_index_in_dim(
+        queries.reshape(row_block, 4, 4, -1), r, axis=2, keepdims=False
+    )
+    outgoing = jnp.transpose(outgoing, (1, 0, 2))
+    q = lax.all_to_all(outgoing, "heads", split_axis=0, concat_axis=0, tiled=True)
+    q = q.reshape(4 * row_block, -1)
+    own = attention(info, start_positions, q, kv_cache, far)
+    by_chip = lax.ppermute(own, "rows", CHIP_SWAP)
+    by_core = lax.ppermute(own, "rows", CORE_SWAP)
+    crossed = lax.ppermute(by_chip, "rows", CORE_SWAP)
+    pieces = (own, by_core, by_chip, crossed)
+
+    columns = out_weight.shape[1]
+    chunk = columns // 4
+    resid = []
+    for first in range(0, columns, chunk):
+        part = project(info, pieces, residual, out_weight, first, chunk)
+        inward = lax.ppermute(part, "heads", TO_CENTRE)
+        side = wide_sum(part, inward).astype(jnp.bfloat16)
+        other = lax.ppermute(side, "heads", CENTRE_SWAP)
+        both = wide_sum(side, other).astype(jnp.bfloat16)
+        outward = lax.ppermute(both, "heads", FROM_CENTRE)
+        resid.append(jnp.where(at_end, outward, both))
+
+    hidden_columns = gate_weight.shape[1]
+    step = 512
+    cuts = [0, hidden_columns // step // 2 * step, hidden_columns]
+    gain = norm_gain[None]
+    inverse = None
+    partial = None
+    for i in range(2):
+        first, width = cuts[i], cuts[i + 1] - cuts[i]
+        keep, send, square = expand(resid, gain, gate_weight, up_weight, first, width, step)
+        got = lax.ppermute(send, "rows", CORE_SWAP)
+        if inverse is None:
+            half = 2 * row_block
+            square = square[:half] + lax.ppermute(square[half:], "rows", CORE_SWAP)
+            square = square[:row_block] + lax.ppermute(square[row_block:], "rows", CHIP_SWAP)
+            inverse = lax.rsqrt(square[:, :1] / D + EPSILON)
+        passed = wide_sum(keep[row_block:], got[row_block:]).astype(jnp.bfloat16)
+        arrived = lax.ppermute(passed, "rows", CHIP_SWAP)
+        total = wide_sum(keep[:row_block], got[:row_block], arrived) * inverse
+        hidden = (jax.nn.silu(total[:, :width]) * total[:, width:]).astype(jnp.bfloat16)
+        hidden_chip = lax.ppermute(hidden, "rows", CHIP_SWAP)
+        hidden_core = lax.ppermute(
+            jnp.concatenate([hidden, hidden_chip], 0), "rows", CORE_SWAP
+        )
+        partial = contract(
+            info, (hidden, hidden_chip, hidden_core), partial, down_weight, first, step
+        )
+    summed = wide_sum(
+        *lax.all_to_all(partial, "heads", split_axis=0, concat_axis=0, tiled=True)
+    )
+    place = (z ^ info[4]) * row_block
+    resid_own = jnp.concatenate(
+        [lax.dynamic_slice_in_dim(piece, place, row_block, 0) for piece in resid], 1
+    )
+    return (resid_own.astype(jnp.float32) + summed).astype(jnp.bfloat16)
+
+
 def solution(mesh):
+    heads, rows = mesh.shape["heads"], mesh.shape["rows"]
+    local = block_local if (heads, rows) == (4, 4) else general_local
     return jax.shard_map(
         local,
         mesh=mesh,

time: 498 us -> 204 us (0.41)
  waiting for transfers between devices: 260 us -> 93.2 us
  blocking collectives: 113 us -> 0 us
  Pallas kernels: 0 us -> 54.8 us
  matrix products: 46.7 us -> 0 us
  between operations: 13.4 us -> 0.48 us
  other arithmetic: 22 us -> 9.38 us
  starting transfers between devices: 21.2 us -> 33.3 us
  local copies, waits for them, and re-layouts: 21.3 us -> 11.5 us
    psum x1 -> x0, waiting for transfers between devices: 129 us -> none  [local(): lax.psum((gate_part, up_part, square), 'rows')]
    psum x2 -> x0, blocking collectives: 80 us -> none  [the longest x1 73.8 us: local(): resid_all = lax.psum(local_term, 'heads').astype(jnp.bfloat16)]
    ppermute x0 -> x26, waiting for transfers between devices: none -> 61.5 us  [the longest x4 20.4 us: block_local(): outward = lax.ppermute(both, 'heads', FROM_CENTRE)]
    pallas_call x0 -> x9, Pallas kernels: none -> 54.8 us  [the longest x2 18.1 us: expand(): pl.pallas_call(functools.partial(expand_kernel, first, step, parts), out_...]
    dot_general x9 -> x0, matrix products: 46.7 us -> none  [the longest x1 13 us: local(): jnp.dot(hidden, down_weight, preferred_element_type=jnp.float32)]
    reduce_scatter x1 -> x0, waiting for transfers between devices: 44 us -> none  [local(): lax.psum_scatter(jnp.dot(hidden, down_weight, preferred_element_type=jnp....]
    all_gather x2 -> x0, blocking collectives: 32.6 us -> none  [merged(): pieces = jax.tree.map(lambda part: lax.all_gather(part, axis), value)]
    all_to_all x5 -> x2, waiting for transfers between devices: 63.8 us -> 31.7 us  [the longest x1 22.9 us: block_local(): lax.all_to_all(partial, 'heads', split_axis=0, concat_axis=0, tiled=True)]
  transfers between devices with their start and end apart: 8 -> 28, of which waited for: 7 -> 16; matrix products, arithmetic and copies ran while one was open for 3% -> 7% of each run, Pallas kernels for 0% -> 14%
where the time goes in v1:
time: 204 us; the launch traced here: 203 us
  waiting for transfers between devices  93.2 us (46%)
  Pallas kernels  54.8 us (27%)
  starting transfers between devices  33.3 us (16%)
  local copies, waits for them, and re-layouts  11.5 us (6%)
  other arithmetic  9.38 us (5%)
    all_to_all x1, waiting for transfers between devices, block_local(): lax.all_to_all(partial, 'heads', split_axis=0, concat_axis=0, tiled=True)  22.9 us
    ppermute x4, waiting for transfers between devices, block_local(): outward = lax.ppermute(both, 'heads', FROM_CENTRE)  20.4 us
    pallas_call x2, Pallas kernels, expand(): pl.pallas_call(functools.partial(expand_kernel, first, step, parts), out_...  18.1 us
    ppermute x2, waiting for transfers between devices, block_local(): arrived = lax.ppermute(passed, 'rows', CHIP_SWAP)  18.1 us
    pallas_call x4, Pallas kernels, project(): pl.pallas_call(functools.partial(project_kernel, first), out_shape=jax.Sh...  15.9 us
    pallas_call x2, Pallas kernels, contract(): pl.pallas_call(functools.partial(contract_kernel, first, step, final), ou...  13.4 us
    all_to_all x1, waiting for transfers between devices, block_local(): lax.all_to_all(outgoing, 'heads', split_axis=0, concat_axis=0, tiled=True)  8.87 us
    ppermute x2, waiting for transfers between devices, block_local(): hidden_chip = lax.ppermute(hidden, 'rows', CHIP_SWAP)  8.49 us
  transfers between devices with their start and end apart: 28, of which 16 were waited for; matrix products, arithmetic and copies ran while one was open for 7% of the time, Pallas kernels for 14%

profile of v1, /device:TPU:0, one launch (start us, length us, event | category | flops | bytes accessed | tf_op | source)
XLA Modules:
  0.0 202.8 jit_solution(14727492314290684421)
XLA Ops:
  0.5 1.8 reshape.13
  2.9 0.9 copy.13
  3.8 5.9 %all-to-all-start = ((bf16[4,64,512]{2,1,0:T(8,128)(2,1)}), bf16[4,64,512]{2,1,0:T(8,128)(2,1)S(1)}, u32[]{:S(2)}, u32[]{:S(2)}) async-start(bf16[4,64,512]{2,1,0:T(8,128)(2,1)} %bitcast.15), calls=%async_computation | async-start | bytes 524288 | tf_op jit(solution)/shard_map/all_to_all | solution.py:422
  9.6 0.7 stack.23.info
  10.3 8.9 %all-to-all-done = bf16[4,64,512]{2,1,0:T(8,128)(2,1)S(1)} async-done(((bf16[4,64,512]{2,1,0:T(8,128)(2,1)}), bf16[4,64,512]{2,1,0:T(8,128)(2,1)S(1)}, u32[]{:S(2)}, u32[]{:S(2)}) %all-to-all-start) | async-done | bytes 262176 | tf_op jit(solution)/shard_map/all_to_all | solution.py:422
  19.2 0.7 copy-done.9
  20.3 7.4 %attention.1.own = bf16[256,512]{1,0:T(8,128)(2,1)} custom-call(s32[5]{0:T(128)} %stack.23.info, s32[2]{0:T(128)} %starts.1, bf16[256,512]{1,0:T(8,128)(2,1)} %bitcast.16, bf16[2,2,1024,128]{3,2,1,0:T(8,128)(2,1)} %near.1, bf16[2,2,1024,128]{3,2,1,0:T(8,128)(2,1)} %copy-done.6), custom_call_target="tpu_custom_call" | custom-call | tf_op jit(solution)/shard_map/attention/pallas_call | solution.py:222
  27.7 1.5 collective-permute-start.2
  29.2 5.1 %collective-permute-done.2.chip = bf16[256,512]{1,0:T(8,128)(2,1)S(1)} collective-permute-done((bf16[256,512]{1,0:T(8,128)(2,1)}, bf16[256,512]{1,0:T(8,128)(2,1)S(1)}, u32[]{:S(2)}, u32[]{:S(2)}) %collective-permute-start.2) | collective-permute-done | bytes 262176 | tf_op jit(solution)/shard_map/ppermute | solution.py:425
  34.3 1.5 collective-permute-done.3.cross
  35.8 0.7 copy-done.2
  36.5 4.0 %project.4 = bf16[256,512]{1,0:T(8,128)(2,1)} custom-call(s32[5]{0:T(128)} %stack.23.info, bf16[256,512]{1,0:T(8,128)(2,1)} %attention.1.own, bf16[256,512]{1,0:T(8,128)(2,1)} %copy-done.1, bf16[256,512]{1,0:T(8,128)(2,1)} %copy-done, bf16[256,512]{1,0:T(8,128)(2,1)} %copy-done.2, bf16[64,2048]{1,0:T(8,128)(2,1)} %residual.7, bf16[2048,2048]{1,0:T(8,128)(2,1)} %w_hbm.7), custom_call_target="tpu_custom_call" | custom-call | tf_op jit(solution)/shard_map/project/pallas_call | solution.py:261
  40.5 3.0 %collective-permute-start.4 = (bf16[256,512]{1,0:T(8,128)(2,1)}, bf16[256,512]{1,0:T(8,128)(2,1)S(1)}, u32[]{:S(2)}, u32[]{:S(2)}) collective-permute-start(bf16[256,512]{1,0:T(8,128)(2,1)} %project.4), channel_id=1, source_target_pairs={{0,4},{12,8},{1,5},{13,9},{2,6},{14,10},{3,7},{15,11},{16,20},{28,... | collective-permute-start | bytes 786440 | tf_op jit(solution)/shard_map/ppermute | solution.py:435
  43.5 4.0 %project.5 = bf16[256,512]{1,0:T(8,128)(2,1)} custom-call(s32[5]{0:T(128)} %stack.23.info, bf16[256,512]{1,0:T(8,128)(2,1)} %attention.1.own, bf16[256,512]{1,0:T(8,128)(2,1)} %copy-done.1, bf16[256,512]{1,0:T(8,128)(2,1)} %copy-done, bf16[256,512]{1,0:T(8,128)(2,1)} %copy-done.2, bf16[64,2048]{1,0:T(8,128)(2,1)} %residual.7, bf16[2048,2048]{1,0:T(8,128)(2,1)} %w_hbm.7), custom_call_target="tpu_custom_call" | custom-call | tf_op jit(solution)/shard_map/project/pallas_call | solution.py:261
  47.5 1.4 collective-permute-start.7
  48.9 4.0 %project.6 = bf16[256,512]{1,0:T(8,128)(2,1)} custom-call(s32[5]{0:T(128)} %stack.23.info, bf16[256,512]{1,0:T(8,128)(2,1)} %attention.1.own, bf16[256,512]{1,0:T(8,128)(2,1)} %copy-done.1, bf16[256,512]{1,0:T(8,128)(2,1)} %copy-done, bf16[256,512]{1,0:T(8,128)(2,1)} %copy-done.2, bf16[64,2048]{1,0:T(8,128)(2,1)} %residual.7, bf16[2048,2048]{1,0:T(8,128)(2,1)} %w_hbm.7), custom_call_target="tpu_custom_call" | custom-call | tf_op jit(solution)/shard_map/project/pallas_call | solution.py:261
  52.9 1.3 collective-permute-start.10
  54.3 4.0 %project.7 = bf16[256,512]{1,0:T(8,128)(2,1)} custom-call(s32[5]{0:T(128)} %stack.23.info, bf16[256,512]{1,0:T(8,128)(2,1)} %attention.1.own, bf16[256,512]{1,0:T(8,128)(2,1)} %copy-done.1, bf16[256,512]{1,0:T(8,128)(2,1)} %copy-done, bf16[256,512]{1,0:T(8,128)(2,1)} %copy-done.2, bf16[64,2048]{1,0:T(8,128)(2,1)} %residual.7, bf16[2048,2048]{1,0:T(8,128)(2,1)} %w_hbm.7), custom_call_target="tpu_custom_call" | custom-call | tf_op jit(solution)/shard_map/project/pallas_call | solution.py:261
  58.2 1.3 collective-permute-start.13
  59.6 0.7 collective-permute-start.5
  60.4 0.7 collective-permute-start.8
  61.4 1.0 add_convert_fusion.5
  62.4 0.7 collective-permute-start.11
  63.1 3.4 %collective-permute-done.13 = bf16[256,512]{1,0:T(8,128)(2,1)S(1)} collective-permute-done((bf16[256,512]{1,0:T(8,128)(2,1)}, bf16[256,512]{1,0:T(8,128)(2,1)S(1)}, u32[]{:S(2)}, u32[]{:S(2)}) %collective-permute-start.13) | collective-permute-done | bytes 262176 | tf_op jit(solution)/shard_map/ppermute | solution.py:435
  66.5 1.0 add_convert_fusion.3
  67.5 0.7 collective-permute-start.14
  68.3 1.3 collective-permute-start.6
  69.7 1.3 collective-permute-start.9
  71.1 1.3 collective-permute-start.12
  72.5 1.5 collective-permute-start.15
  73.9 7.4 %collective-permute-done.6 = bf16[256,512]{1,0:T(8,128)(2,1)S(1)} collective-permute-done((bf16[256,512]{1,0:T(8,128)(2,1)S(1)}, bf16[256,512]{1,0:T(8,128)(2,1)S(1)}, u32[]{:S(2)}, u32[]{:S(2)}) %collective-permute-start.6) | collective-permute-done | bytes 262176 | tf_op jit(solution)/shard_map/ppermute | solution.py:439
  81.3 0.7 broadcast_select_fusion.3.refs_0_
  82.1 4.9 %collective-permute-done.9 = bf16[256,512]{1,0:T(8,128)(2,1)S(1)} collective-permute-done((bf16[256,512]{1,0:T(8,128)(2,1)S(1)}, bf16[256,512]{1,0:T(8,128)(2,1)S(1)}, u32[]{:S(2)}, u32[]{:S(2)}) %collective-permute-start.9) | collective-permute-done | bytes 262176 | tf_op jit(solution)/shard_map/ppermute | solution.py:439
  87.0 0.7 broadcast_select_fusion.2.refs_1_
  87.7 4.9 %collective-permute-done.12 = bf16[256,512]{1,0:T(8,128)(2,1)S(1)} collective-permute-done((bf16[256,512]{1,0:T(8,128)(2,1)S(1)}, bf16[256,512]{1,0:T(8,128)(2,1)S(1)}, u32[]{:S(2)}, u32[]{:S(2)}) %collective-permute-start.12) | collective-permute-done | bytes 262176 | tf_op jit(solution)/shard_map/ppermute | solution.py:439
  92.6 0.7 broadcast_select_fusion.1.refs_2_
  93.3 3.2 %collective-permute-done.15 = bf16[256,512]{1,0:T(8,128)(2,1)S(1)} collective-permute-done((bf16[256,512]{1,0:T(8,128)(2,1)S(1)}, bf16[256,512]{1,0:T(8,128)(2,1)S(1)}, u32[]{:S(2)}, u32[]{:S(2)}) %collective-permute-start.15) | collective-permute-done | bytes 262176 | tf_op jit(solution)/shard_map/ppermute | solution.py:439
  96.5 0.7 broadcast_select_fusion.refs_3_
  97.3 8.3 %expand.3 = (bf16[128,3072]{1,0:T(8,128)(2,1)}, bf16[128,3072]{1,0:T(8,128)(2,1)}, f32[256,128]{1,0:T(8,128)}) custom-call(f32[1,2048]{1,0:T(1,128)} %bitcast.17, bf16[256,512]{1,0:T(8,128)(2,1)} %broadcast_select_fusion.3.refs_0_, bf16[256,512]{1,0:T(8,128)(2,1)} %broadcast_select_fusion.2.refs_1_, bf16[256,512]{1,0:T(8,128)(2,1)} %broadcast_select_fusion.1.refs_2_, ...), custom_call_target="tpu_custom_call" | custom-call | tf_op jit(solution)/shard_map/expand/pallas_call | solution.py:313
  105.6 0.8 slice.56
  107.0 9.9 %expand.2 = (bf16[128,4096]{1,0:T(8,128)(2,1)}, bf16[128,4096]{1,0:T(8,128)(2,1)}, f32[256,128]{1,0:T(8,128)}) custom-call(f32[1,2048]{1,0:T(1,128)} %bitcast.18, bf16[256,512]{1,0:T(8,128)(2,1)} %broadcast_select_fusion.3.refs_0_, bf16[256,512]{1,0:T(8,128)(2,1)} %broadcast_select_fusion.2.refs_1_, bf16[256,512]{1,0:T(8,128)(2,1)} %broadcast_select_fusion.1.refs_2_, ...), custom_call_target="tpu_custom_call" | custom-call | tf_op jit(solution)/shard_map/expand/pallas_call | solution.py:313
  117.1 1.6 collective-permute-start.19
  118.6 2.4 %collective-permute-done.19 = f32[64,128]{1,0:T(8,128)S(1)} collective-permute-done((f32[64,128]{1,0:T(8,128)S(1)}, f32[64,128]{1,0:T(8,128)S(1)}, u32[]{:S(2)}, u32[]{:S(2)}) %collective-permute-start.19) | collective-permute-done | bytes 32800 | tf_op jit(solution)/shard_map/ppermute | solution.py:455
  121.3 1.6 collective-permute-start.23
  122.8 1.2 add_convert_fusion
  124.0 0.6 collective-permute-start.17
  124.6 8.7 %collective-permute-done.23 = bf16[64,3072]{1,0:T(8,128)(2,1)S(1)} collective-permute-done((bf16[64,3072]{1,0:T(8,128)(2,1)S(1)}, bf16[64,3072]{1,0:T(8,128)(2,1)S(1)}, u32[]{:S(2)}, u32[]{:S(2)}) %collective-permute-start.23) | collective-permute-done | bytes 393248 | tf_op jit(solution)/shard_map/ppermute | solution.py:458
  133.5 9.4 %collective-permute-done.17 = bf16[64,4096]{1,0:T(8,128)(2,1)S(1)} collective-permute-done((bf16[64,4096]{1,0:T(8,128)(2,1)S(1)}, bf16[64,4096]{1,0:T(8,128)(2,1)S(1)}, u32[]{:S(2)}, u32[]{:S(2)}) %collective-permute-start.17) | collective-permute-done | bytes 524320 | tf_op jit(solution)/shard_map/ppermute | solution.py:458
  142.9 1.3 add_multiply_fusion
  144.3 1.6 collective-permute-start.20
  146.6 6.5 %collective-permute-done.20.refs_1_ = bf16[64,2048]{1,0:T(8,128)(2,1)S(1)} collective-permute-done((bf16[64,2048]{1,0:T(8,128)(2,1)S(1)}, bf16[64,2048]{1,0:T(8,128)(2,1)S(1)}, u32[]{:S(2)}, u32[]{:S(2)}) %collective-permute-start.20) | collective-permute-done | bytes 262176 | tf_op jit(solution)/shard_map/ppermute | solution.py:461
  153.2 2.0 collective-permute-done.24.refs_1_
  155.3 1.7 collective-permute-done.25.refs_2_
  157.0 0.8 copy-done.13
  157.8 6.2 %contract.2.refs_3_ = f32[256,2048]{1,0:T(8,128)} custom-call(s32[5]{0:T(128)} %stack.23.info, bf16[64,1536]{1,0:T(8,128)(2,1)} %copy-done.4, bf16[64,1536]{1,0:T(8,128)(2,1)} %copy-done.10, bf16[128,1536]{1,0:T(8,128)(2,1)} %copy-done.13, bf16[3584,2048]{1,0:T(8,128)(2,1)} %refs_4_.5), custom_call_target="tpu_custom_call" | custom-call | tf_op jit(solution)/shard_map/contract/pallas_call | solution.py:381
  164.0 0.8 copy-done.12
  164.8 7.3 %contract.3 = bf16[4,64,2048]{2,1,0:T(8,128)(2,1)} custom-call(s32[5]{0:T(128)} %stack.23.info, bf16[64,2048]{1,0:T(8,128)(2,1)} %copy-done.3, bf16[64,2048]{1,0:T(8,128)(2,1)} %copy-done.5, bf16[128,2048]{1,0:T(8,128)(2,1)} %copy-done.12, f32[256,2048]{1,0:T(8,128)} %contract.2.refs_3_, bf16[3584,2048]{1,0:T(8,128)(2,1)} %refs_4_.5), custom_call_target="tpu_custom_call" | custom-call | tf_op jit(solution)/shard_map/contract/pallas_call | solution.py:381
  172.1 3.5 %all-to-all-start.1 = ((bf16[4,64,2048]{2,1,0:T(8,128)(2,1)}), bf16[4,64,2048]{2,1,0:T(8,128)(2,1)S(1)}, u32[]{:S(2)}, u32[]{:S(2)}) async-start(bf16[4,64,2048]{2,1,0:T(8,128)(2,1)} %contract.3), calls=%async_computation.1 | async-start | bytes 2097152 | tf_op jit(solution)/shard_map/all_to_all | solution.py:469
  175.6 0.8 constant_dynamic-slice_fusion.3
  176.5 0.8 constant_dynamic-slice_fusion.2
  177.3 0.8 constant_dynamic-slice_fusion.1
  178.2 0.8 constant_dynamic-slice_fusion
  179.0 22.9 %all-to-all-done.1 = bf16[4,64,2048]{2,1,0:T(8,128)(2,1)S(1)} async-done(((bf16[4,64,2048]{2,1,0:T(8,128)(2,1)}), bf16[4,64,2048]{2,1,0:T(8,128)(2,1)S(1)}, u32[]{:S(2)}, u32[]{:S(2)}) %all-to-all-start.1) | async-done | bytes 1048608 | tf_op jit(solution)/shard_map/all_to_all | solution.py:469
  201.9 0.9 fusion.1
  (64 shorter events, 4.5 us)
Async XLA Ops:
  0.0 19.2 %collective-permute-start = (bf16[2,2,1024,128]{3,2,1,0:T(8,128)(2,1)}, bf16[2,2,1024,128]{3,2,1,0:T(8,128)(2,1)S(1)}, u32[]{:S(2)}, u32[]{:S(2)}) collective-permute-start(bf16[2,2,1024,128]{3,2,1,0:T(8,128)(2,1)} %near.1), channel_id=1, source_target_pairs={{0,1},{1,0},{2,3},{3,2},{4,5},{5,4},{6,7},{7,6},{8,9},{9,8},{10,11... | collective-permute-start | bytes 3145736 | tf_op jit(solution)/shard_map/ppermute | solution.py:417
  3.8 15.4 %all-to-all-start = ((bf16[4,64,512]{2,1,0:T(8,128)(2,1)}), bf16[4,64,512]{2,1,0:T(8,128)(2,1)S(1)}, u32[]{:S(2)}, u32[]{:S(2)}) async-start(bf16[4,64,512]{2,1,0:T(8,128)(2,1)} %bitcast.15), calls=%async_computation | async-start | bytes 524288 | tf_op jit(solution)/shard_map/all_to_all | solution.py:422
  19.2 0.7 copy-start.9
  19.2 1.1 copy-start.6
  27.7 6.6 %collective-permute-start.2 = (bf16[256,512]{1,0:T(8,128)(2,1)}, bf16[256,512]{1,0:T(8,128)(2,1)S(1)}, u32[]{:S(2)}, u32[]{:S(2)}) collective-permute-start(bf16[256,512]{1,0:T(8,128)(2,1)} %attention.1.own), channel_id=1, source_target_pairs={{0,2},{2,0},{1,3},{3,1},{4,6},{6,4},{5,7},{7,5},{8,10},{10,8},{9,1... | collective-permute-start | bytes 786440 | tf_op jit(solution)/shard_map/ppermute | solution.py:425
  29.2 5.1 %collective-permute-start.1 = (bf16[256,512]{1,0:T(8,128)(2,1)}, bf16[256,512]{1,0:T(8,128)(2,1)S(1)}, u32[]{:S(2)}, u32[]{:S(2)}) collective-permute-start(bf16[256,512]{1,0:T(8,128)(2,1)} %attention.1.own), channel_id=1, source_target_pairs={{0,1},{1,0},{2,3},{3,2},{4,5},{5,4},{6,7},{7,6},{8,9},{9,8},{10,11... | collective-permute-start | bytes 786440 | tf_op jit(solution)/shard_map/ppermute | solution.py:426
  34.3 1.5 copy-start
  34.3 1.5 collective-permute-start.3
  34.3 1.5 copy-start.1
  35.8 0.7 copy-start.2
  40.5 19.0 %copy-start.8 = (bf16[256,512]{1,0:T(8,128)(2,1)S(1)}, bf16[256,512]{1,0:T(8,128)(2,1)}, u32[]{:S(2)}) copy-start(bf16[256,512]{1,0:T(8,128)(2,1)} %project.4) | copy-start | bytes 786436
  40.5 19.0 %collective-permute-start.4 = (bf16[256,512]{1,0:T(8,128)(2,1)}, bf16[256,512]{1,0:T(8,128)(2,1)S(1)}, u32[]{:S(2)}, u32[]{:S(2)}) collective-permute-start(bf16[256,512]{1,0:T(8,128)(2,1)} %project.4), channel_id=1, source_target_pairs={{0,4},{12,8},{1,5},{13,9},{2,6},{14,10},{3,7},{15,11},{16,20},{28,... | collective-permute-start | bytes 786440 | tf_op jit(solution)/shard_map/ppermute | solution.py:435
  47.5 12.8 %copy-start.7 = (bf16[256,512]{1,0:T(8,128)(2,1)S(1)}, bf16[256,512]{1,0:T(8,128)(2,1)}, u32[]{:S(2)}) copy-start(bf16[256,512]{1,0:T(8,128)(2,1)} %project.5) | copy-start | bytes 786436
  47.5 12.8 %collective-permute-start.7 = (bf16[256,512]{1,0:T(8,128)(2,1)}, bf16[256,512]{1,0:T(8,128)(2,1)S(1)}, u32[]{:S(2)}, u32[]{:S(2)}) collective-permute-start(bf16[256,512]{1,0:T(8,128)(2,1)} %project.5), channel_id=1, source_target_pairs={{0,4},{12,8},{1,5},{13,9},{2,6},{14,10},{3,7},{15,11},{16,20},{28,... | collective-permute-start | bytes 786440 | tf_op jit(solution)/shard_map/ppermute | solution.py:435
  52.9 8.5 %collective-permute-start.10 = (bf16[256,512]{1,0:T(8,128)(2,1)}, bf16[256,512]{1,0:T(8,128)(2,1)S(1)}, u32[]{:S(2)}, u32[]{:S(2)}) collective-permute-start(bf16[256,512]{1,0:T(8,128)(2,1)} %project.6), channel_id=1, source_target_pairs={{0,4},{12,8},{1,5},{13,9},{2,6},{14,10},{3,7},{15,11},{16,20},{28,... | collective-permute-start | bytes 786440 | tf_op jit(solution)/shard_map/ppermute | solution.py:435
  58.2 8.3 %collective-permute-start.13 = (bf16[256,512]{1,0:T(8,128)(2,1)}, bf16[256,512]{1,0:T(8,128)(2,1)S(1)}, u32[]{:S(2)}, u32[]{:S(2)}) collective-permute-start(bf16[256,512]{1,0:T(8,128)(2,1)} %project.7), channel_id=1, source_target_pairs={{0,4},{12,8},{1,5},{13,9},{2,6},{14,10},{3,7},{15,11},{16,20},{28,... | collective-permute-start | bytes 786440 | tf_op jit(solution)/shard_map/ppermute | solution.py:435
  59.6 8.6 %collective-permute-start.5 = (bf16[256,512]{1,0:T(8,128)(2,1)S(1)}, bf16[256,512]{1,0:T(8,128)(2,1)S(1)}, u32[]{:S(2)}, u32[]{:S(2)}) collective-permute-start(bf16[256,512]{1,0:T(8,128)(2,1)S(1)} %add_convert_fusion.9), channel_id=1, source_target_pairs={{4,8},{8,4},{5,9},{9,5},{6,10},{10,6},{7,11},{11,7},{20,24},{24,20... | collective-permute-start | bytes 786440 | tf_op jit(solution)/shard_map/ppermute | solution.py:437
  60.4 9.2 %collective-permute-start.8 = (bf16[256,512]{1,0:T(8,128)(2,1)S(1)}, bf16[256,512]{1,0:T(8,128)(2,1)S(1)}, u32[]{:S(2)}, u32[]{:S(2)}) collective-permute-start(bf16[256,512]{1,0:T(8,128)(2,1)S(1)} %add_convert_fusion.7), channel_id=1, source_target_pairs={{4,8},{8,4},{5,9},{9,5},{6,10},{10,6},{7,11},{11,7},{20,24},{24,20... | collective-permute-start | bytes 786440 | tf_op jit(solution)/shard_map/ppermute | solution.py:437
  62.4 8.6 %collective-permute-start.11 = (bf16[256,512]{1,0:T(8,128)(2,1)S(1)}, bf16[256,512]{1,0:T(8,128)(2,1)S(1)}, u32[]{:S(2)}, u32[]{:S(2)}) collective-permute-start(bf16[256,512]{1,0:T(8,128)(2,1)S(1)} %add_convert_fusion.5), channel_id=1, source_target_pairs={{4,8},{8,4},{5,9},{9,5},{6,10},{10,6},{7,11},{11,7},{20,24},{24,20... | collective-permute-start | bytes 786440 | tf_op jit(solution)/shard_map/ppermute | solution.py:437
  67.5 4.8 %collective-permute-start.14 = (bf16[256,512]{1,0:T(8,128)(2,1)S(1)}, bf16[256,512]{1,0:T(8,128)(2,1)S(1)}, u32[]{:S(2)}, u32[]{:S(2)}) collective-permute-start(bf16[256,512]{1,0:T(8,128)(2,1)S(1)} %add_convert_fusion.3), channel_id=1, source_target_pairs={{4,8},{8,4},{5,9},{9,5},{6,10},{10,6},{7,11},{11,7},{20,24},{24,20... | collective-permute-start | bytes 786440 | tf_op jit(solution)/shard_map/ppermute | solution.py:437
  68.3 13.0 %collective-permute-start.6 = (bf16[256,512]{1,0:T(8,128)(2,1)S(1)}, bf16[256,512]{1,0:T(8,128)(2,1)S(1)}, u32[]{:S(2)}, u32[]{:S(2)}) collective-permute-start(bf16[256,512]{1,0:T(8,128)(2,1)S(1)} %add_convert_fusion.8), channel_id=1, source_target_pairs={{4,0},{8,12},{5,1},{9,13},{6,2},{10,14},{7,3},{11,15},{20,16},{24,... | collective-permute-start | bytes 786440 | tf_op jit(solution)/shard_map/ppermute | solution.py:439
  69.7 17.3 %collective-permute-start.9 = (bf16[256,512]{1,0:T(8,128)(2,1)S(1)}, bf16[256,512]{1,0:T(8,128)(2,1)S(1)}, u32[]{:S(2)}, u32[]{:S(2)}) collective-permute-start(bf16[256,512]{1,0:T(8,128)(2,1)S(1)} %add_convert_fusion.6), channel_id=1, source_target_pairs={{4,0},{8,12},{5,1},{9,13},{6,2},{10,14},{7,3},{11,15},{20,16},{24,... | collective-permute-start | bytes 786440 | tf_op jit(solution)/shard_map/ppermute | solution.py:439
  71.1 21.5 %collective-permute-start.12 = (bf16[256,512]{1,0:T(8,128)(2,1)S(1)}, bf16[256,512]{1,0:T(8,128)(2,1)S(1)}, u32[]{:S(2)}, u32[]{:S(2)}) collective-permute-start(bf16[256,512]{1,0:T(8,128)(2,1)S(1)} %add_convert_fusion.4), channel_id=1, source_target_pairs={{4,0},{8,12},{5,1},{9,13},{6,2},{10,14},{7,3},{11,15},{20,16},{24,... | collective-permute-start | bytes 786440 | tf_op jit(solution)/shard_map/ppermute | solution.py:439
  72.5 24.1 %collective-permute-start.15 = (bf16[256,512]{1,0:T(8,128)(2,1)S(1)}, bf16[256,512]{1,0:T(8,128)(2,1)S(1)}, u32[]{:S(2)}, u32[]{:S(2)}) collective-permute-start(bf16[256,512]{1,0:T(8,128)(2,1)S(1)} %add_convert_fusion.2), channel_id=1, source_target_pairs={{4,0},{8,12},{5,1},{9,13},{6,2},{10,14},{7,3},{11,15},{20,16},{24,... | collective-permute-start | bytes 786440 | tf_op jit(solution)/shard_map/ppermute | solution.py:439
  105.5 15.6 %collective-permute-start.22 = (bf16[128,3072]{1,0:T(8,128)(2,1)}, bf16[128,3072]{1,0:T(8,128)(2,1)S(1)}, u32[]{:S(2)}, u32[]{:S(2)}) collective-permute-start(bf16[128,3072]{1,0:T(8,128)(2,1)} %get-tuple-element.14), channel_id=1, source_target_pairs={{0,1},{1,0},{2,3},{3,2},{4,5},{5,4},{6,7},{7,6},{8,9},{9,8},{10,11... | collective-permute-start | bytes 2359304 | tf_op jit(solution)/shard_map/ppermute | solution.py:451
  106.4 10.6 %copy-start.14 = (f32[256,128]{1,0:T(8,128)S(1)}, f32[256,128]{1,0:T(8,128)}, u32[]{:S(2)}) copy-start(f32[256,128]{1,0:T(8,128)} %get-tuple-element.12) | copy-start | bytes 393220
  106.4 14.7 %copy-start.11 = (bf16[128,3072]{1,0:T(8,128)(2,1)S(1)}, bf16[128,3072]{1,0:T(8,128)(2,1)}, u32[]{:S(2)}) copy-start(bf16[128,3072]{1,0:T(8,128)(2,1)} %get-tuple-element.13) | copy-start | bytes 2359300
  106.5 10.6 %collective-permute-start.18 = (f32[128,128]{1,0:T(8,128)S(1)}, f32[128,128]{1,0:T(8,128)S(1)}, u32[]{:S(2)}, u32[]{:S(2)}) collective-permute-start(f32[128,128]{1,0:T(8,128)S(1)} %slice.56), channel_id=1, source_target_pairs={{0,1},{1,0},{2,3},{3,2},{4,5},{5,4},{6,7},{7,6},{8,9},{9,8},{10,11... | collective-permute-start | bytes 196616 | tf_op jit(solution)/shard_map/ppermute | solution.py:454
  116.9 6.0 %collective-permute-start.16 = (bf16[128,4096]{1,0:T(8,128)(2,1)}, bf16[128,4096]{1,0:T(8,128)(2,1)S(1)}, u32[]{:S(2)}, u32[]{:S(2)}) collective-permute-start(bf16[128,4096]{1,0:T(8,128)(2,1)} %get-tuple-element.11), channel_id=1, source_target_pairs={{0,1},{1,0},{2,3},{3,2},{4,5},{5,4},{6,7},{7,6},{8,9},{9,8},{10,11... | collective-permute-start | bytes 3145736 | tf_op jit(solution)/shard_map/ppermute | solution.py:451
  117.1 4.0 %collective-permute-start.19 = (f32[64,128]{1,0:T(8,128)S(1)}, f32[64,128]{1,0:T(8,128)S(1)}, u32[]{:S(2)}, u32[]{:S(2)}) collective-permute-start(f32[64,128]{1,0:T(8,128)S(1)} %get-tuple-element.16), channel_id=1, source_target_pairs={{0,2},{2,0},{1,3},{3,1},{4,6},{6,4},{5,7},{7,5},{8,10},{10,8},{9,1... | collective-permute-start | bytes 98312 | tf_op jit(solution)/shard_map/ppermute | solution.py:455
  121.3 12.1 %collective-permute-start.23 = (bf16[64,3072]{1,0:T(8,128)(2,1)S(1)}, bf16[64,3072]{1,0:T(8,128)(2,1)S(1)}, u32[]{:S(2)}, u32[]{:S(2)}) collective-permute-start(bf16[64,3072]{1,0:T(8,128)(2,1)S(1)} %add_convert_fusion.1), channel_id=1, source_target_pairs={{0,2},{2,0},{1,3},{3,1},{4,6},{6,4},{5,7},{7,5},{8,10},{10,8},{9,1... | collective-permute-start | bytes 1179656 | tf_op jit(solution)/shard_map/ppermute | solution.py:458
  124.0 18.9 %collective-permute-start.17 = (bf16[64,4096]{1,0:T(8,128)(2,1)S(1)}, bf16[64,4096]{1,0:T(8,128)(2,1)S(1)}, u32[]{:S(2)}, u32[]{:S(2)}) collective-permute-start(bf16[64,4096]{1,0:T(8,128)(2,1)S(1)} %add_convert_fusion), channel_id=1, source_target_pairs={{0,2},{2,0},{1,3},{3,1},{4,6},{6,4},{5,7},{7,5},{8,10},{10,8},{9,1... | collective-permute-start | bytes 1572872 | tf_op jit(solution)/shard_map/ppermute | solution.py:458
  144.3 19.7 %copy-start.3 = (bf16[64,2048]{1,0:T(8,128)(2,1)}, bf16[64,2048]{1,0:T(8,128)(2,1)S(1)}, u32[]{:S(2)}) copy-start(bf16[64,2048]{1,0:T(8,128)(2,1)S(1)} %fusion.refs_0_) | copy-start | bytes 786436
  144.3 8.8 %collective-permute-start.20 = (bf16[64,2048]{1,0:T(8,128)(2,1)S(1)}, bf16[64,2048]{1,0:T(8,128)(2,1)S(1)}, u32[]{:S(2)}, u32[]{:S(2)}) collective-permute-start(bf16[64,2048]{1,0:T(8,128)(2,1)S(1)} %fusion.refs_0_), channel_id=1, source_target_pairs={{0,2},{2,0},{1,3},{3,1},{4,6},{6,4},{5,7},{7,5},{8,10},{10,8},{9,1... | collective-permute-start | bytes 786440 | tf_op jit(solution)/shard_map/ppermute | solution.py:461
  146.0 11.0 %copy-start.4 = (bf16[64,1536]{1,0:T(8,128)(2,1)}, bf16[64,1536]{1,0:T(8,128)(2,1)S(1)}, u32[]{:S(2)}) copy-start(bf16[64,1536]{1,0:T(8,128)(2,1)S(1)} %fusion.2.refs_0_) | copy-start | bytes 589828
  146.0 9.2 %collective-permute-start.24 = (bf16[64,1536]{1,0:T(8,128)(2,1)S(1)}, bf16[64,1536]{1,0:T(8,128)(2,1)S(1)}, u32[]{:S(2)}, u32[]{:S(2)}) collective-permute-start(bf16[64,1536]{1,0:T(8,128)(2,1)S(1)} %fusion.2.refs_0_), channel_id=1, source_target_pairs={{0,2},{2,0},{1,3},{3,1},{4,6},{6,4},{5,7},{7,5},{8,10},{10,8},{9,1... | collective-permute-start | bytes 589832 | tf_op jit(solution)/shard_map/ppermute | solution.py:461
  153.1 10.9 %copy-start.5 = (bf16[64,2048]{1,0:T(8,128)(2,1)}, bf16[64,2048]{1,0:T(8,128)(2,1)S(1)}, u32[]{:S(2)}) copy-start(bf16[64,2048]{1,0:T(8,128)(2,1)S(1)} %collective-permute-done.20.refs_1_) | copy-start | bytes 786436
  153.2 10.8 %collective-permute-start.21 = (bf16[128,2048]{1,0:T(8,128)(2,1)S(1)}, bf16[128,2048]{1,0:T(8,128)(2,1)S(1)}, u32[]{:S(2)}, u32[]{:S(2)}) collective-permute-start(bf16[128,2048]{1,0:T(8,128)(2,1)S(1)} %pad_maximum_fusion), channel_id=1, source_target_pairs={{0,1},{1,0},{2,3},{3,2},{4,5},{5,4},{6,7},{7,6},{8,9},{9,8},{10,11... | collective-permute-start | bytes 1572872 | tf_op jit(solution)/shard_map/ppermute | solution.py:462
  155.2 1.8 copy-start.10
  155.3 1.8 collective-permute-start.25
  157.0 0.8 copy-start.13
  164.0 0.8 copy-start.12
  172.1 29.8 %all-to-all-start.1 = ((bf16[4,64,2048]{2,1,0:T(8,128)(2,1)}), bf16[4,64,2048]{2,1,0:T(8,128)(2,1)S(1)}, u32[]{:S(2)}, u32[]{:S(2)}) async-start(bf16[4,64,2048]{2,1,0:T(8,128)(2,1)} %contract.3), calls=%async_computation.1 | async-start | bytes 2097152 | tf_op jit(solution)/shard_map/all_to_all | solution.py:469
